TPU v7x, 256 devices: a whole 4x4x8 slice. The times are simulated.
256 devices in a mesh: sky: 32 (over z_hi, y, core), exp: 8 (over z_lo, x).
Axes of the slice: x: 4, y: 4, z: 8 (z_hi: 4, z_lo: 2; z = z_hi * 2 + z_lo), core: 2. Of those that a mesh axis runs over, the one named last changes fastest.
Arguments:
- warped: bfloat16 [16, 3840, 1024], P('exp', 'sky'), may hold values from -6 to 6
- variance: bfloat16 [16, 3840, 1024], P('exp', 'sky'), may hold values from 0.5 to 8
- basis_taps: bfloat16 [9, 2, 23], replicated, may hold values from -1.25 to 1.25
- coeffs: float32 [16, 9, 10], P('exp'), may hold values from -6 to 6
- degrees: int32 [16, 9], P('exp'), may hold values from 0 to 3
- footprint: int32 [16, 2], P('exp'), may hold values from 0 to 3840, as said below
- masks: int32 [16, 256], P('exp', 'sky'), may hold values from 0 to 1073741823
Outputs:
- coadd: float32 [3840, 1024], P('sky', 'exp')
Inputs may be any that keep to these rules, and one draw needn't show every extreme that they name: Each exposure covers rows footprint[e, 0] up to but not including footprint[e, 1], a nonempty range.
All inputs are finite; a program needn't handle non-finite values.
Results may differ from a plain program's by a relative error of at most 0.0039.
Values may be sent and summed in bfloat16 or wider, within the bound.
A program may use at most 64 MiB of HBM per device.

v0:
```python
import jax
import jax.numpy as jnp
from jax import lax
from jax.sharding import PartitionSpec as P

HIGHEST = lax.Precision.HIGHEST
POWERS = ((0, 0), (1, 0), (0, 1), (2, 0), (1, 1), (0, 2), (3, 0), (2, 1), (1, 2), (0, 3))


def padded_2(cells, sides, width):
    for axis, dim in sides:
        count = lax.axis_size(axis)
        ends = count - 1
        head = lax.slice_in_dim(cells, 0, width, axis=dim)
        tail = lax.slice_in_dim(cells, cells.shape[dim] - width, cells.shape[dim], axis=dim)
        cells = jnp.concatenate(
            [
                lax.ppermute(tail, axis, [(i, (i + 1) % count) for i in range(ends)]),
                cells,
                lax.ppermute(head, axis, [((i + 1) % count, i) for i in range(ends)]),
            ],
            axis=dim,
        )
    return cells


def monomials(total_rows, total_cols, row_start, row_count):
    row_pos = (
        2.0 * (row_start + jnp.arange(row_count, dtype=jnp.int32)).astype(jnp.float32) + 1.0
    ) / total_rows - 1.0
    col_pos = (
        2.0 * jnp.arange(total_cols, dtype=jnp.int32).astype(jnp.float32) + 1.0
    ) / total_cols - 1.0
    return jnp.stack([(row_pos**p)[:, None] * (col_pos**q)[None, :] for p, q in POWERS])


def term_active(degree):
    orders = jnp.array([p + q for p, q in POWERS], dtype=jnp.int32)
    return (orders[None, :] <= degree[:, None]).astype(jnp.float32)


def pixel_weight(bounds, words, var_field, global_rows, local_rows):
    covered = ((global_rows >= bounds[0]) & (global_rows < bounds[1])).astype(jnp.float32)
    per_row = jnp.repeat(words, 15, total_repeat_length=local_rows.shape[0])
    offset = 2 * (local_rows % 15)
    lower = jnp.right_shift(per_row, offset) & 1
    upper = jnp.right_shift(per_row, offset + 1) & 1
    usable = (1 - lower * upper).astype(jnp.float32)
    return (covered * usable)[:, None] / var_field.astype(jnp.float32)


def body(warped, variance, basis_taps, coeffs, degrees, footprint, masks):
    exp_count, row_count, col_count = warped.shape
    basis_count = basis_taps.shape[0]
    tap_count = basis_taps.shape[2]
    half_width = tap_count // 2
    total_rows = row_count * lax.axis_size("sky")
    row_start = lax.axis_index("sky") * row_count
    strips = padded_2(warped, (("sky", 1),), half_width)
    tap_values = basis_taps.astype(jnp.float32)
    out_rows = jnp.arange(row_count, dtype=jnp.int32)[:, None]
    in_rows = jnp.arange(row_count + 2 * half_width, dtype=jnp.int32)[None, :]
    tap_index = jnp.arange(tap_count, dtype=jnp.int32)
    row_onehot = ((in_rows - out_rows)[:, :, None] == tap_index[None, None, :]).astype(jnp.float32)
    row_band = jnp.einsum("ihk,bk->bih", row_onehot, tap_values[:, 0, :], precision=HIGHEST).astype(
        jnp.bfloat16
    )
    window_pos = jnp.arange(256, dtype=jnp.int32)[:, None]
    block_pos = jnp.arange(128, dtype=jnp.int32)[None, :]
    col_onehot = (
        (window_pos - block_pos - 64 + half_width)[:, :, None] == tap_index[None, None, :]
    ).astype(jnp.float32)
    col_band = jnp.einsum("kcj,bj->bkc", col_onehot, tap_values[:, 1, :], precision=HIGHEST).astype(
        jnp.bfloat16
    )
    terms_field = monomials(total_rows, col_count, row_start, row_count)
    local_rows = jnp.arange(row_count, dtype=jnp.int32)
    global_rows = row_start + local_rows
    block_count = col_count // 128

    def first_pass(carry, item):
        image, coef, degree, bounds, words, var_field = item
        along_rows = jnp.einsum(
            "bih,hc->bic", row_band, image, preferred_element_type=jnp.float32
        ).astype(jnp.bfloat16)
        padded = jnp.pad(along_rows, ((0, 0), (0, 0), (64, 64))).reshape(
            basis_count, row_count, block_count + 1, 128
        )
        windows = jnp.concatenate([padded[:, :, :-1, :], padded[:, :, 1:, :]], axis=-1)
        along_cols = jnp.einsum(
            "brjk,bkc->brjc", windows, col_band, preferred_element_type=jnp.float32
        ).reshape(basis_count, row_count, col_count)
        field = jnp.einsum(
            "bt,trc->brc", coef * term_active(degree), terms_field, precision=HIGHEST
        )
        matched = jnp.sum(field * along_cols, axis=0).astype(jnp.bfloat16)
        weight = pixel_weight(bounds, words, var_field, global_rows, local_rows)
        values = matched.astype(jnp.float32)
        return ((carry[0] + weight * values, carry[1] + weight), (matched, weight))

    start = (
        jnp.zeros((row_count, col_count), jnp.float32),
        jnp.zeros((row_count, col_count), jnp.float32),
    )
    (num_first, den_first), (matched_all, weight_all) = lax.scan(
        first_pass, start, (strips, coeffs, degrees, footprint, masks, variance)
    )
    num_whole, den_whole = lax.psum((num_first, den_first), "exp")
    first = num_whole / (1.0 + den_whole)
    values = matched_all.astype(jnp.float32)
    excess = values - first[None, :, :]
    robust = weight_all / (1.0 + excess * excess / (9.0 * variance.astype(jnp.float32)))
    num_final = jnp.sum(robust * values, axis=0)
    den_final = jnp.sum(robust, axis=0)
    num_part, den_part = (
        lax.psum_scatter(num_final, "exp", scatter_dimension=1, tiled=True),
        lax.psum_scatter(den_final, "exp", scatter_dimension=1, tiled=True),
    )
    return num_part / (1.0 + den_part)


def solution(mesh):
    in_specs = (
        P("exp", "sky", None),
        P("exp", "sky", None),
        P(),
        P("exp", None, None),
        P("exp", None),
        P("exp", None),
        P("exp", "sky"),
    )
    out_specs = P("sky", "exp")
    return jax.shard_map(body, mesh=mesh, in_specs=in_specs, out_specs=out_specs, check_vma=False)
```

profile of v0, /device:TPU:64, one launch (start us, length us, event | category | flops | bytes accessed | tf_op | source)
XLA Modules:
  0.0 316.6 jit_solution(2150271567359927428)
XLA Ops:
  6.5 0.9 fusion.46
  7.4 1.9 collective-permute-start
  9.4 6.7 %collective-permute-start.1 = (bf16[2,11,1024]{2,1,0:T(8,128)(2,1)S(1)}, bf16[2,11,1024]{2,1,0:T(8,128)(2,1)S(1)}, u32[]{:S(2)}, u32[]{:S(2)}) collective-permute-start(bf16[2,11,1024]{2,1,0:T(8,128)(2,1)S(1)} %get-tuple-element.708), channel_id=1, source_target_pairs={{8,0},{16,8},{24,16},{32,24},{40,32},{48,40},{56,48},{64,56},{72,6... | collective-permute-start | bytes 135176 | tf_op jit(solution)/shard_map/ppermute | solution.py:20
  16.0 0.9 broadcast_dynamic-update-slice_fusion.6
  17.0 0.9 broadcast_dynamic-update-slice_fusion.5
  17.9 0.8 broadcast_dynamic-update-slice_fusion.4
  18.8 0.9 broadcast_dynamic-update-slice_fusion.3
  19.7 0.9 multiply_dynamic-update-slice_fusion.2
  20.6 0.8 broadcast_dynamic-update-slice_fusion.2
  21.4 0.9 broadcast_dynamic-update-slice_fusion.1
  22.3 0.9 multiply_dynamic-update-slice_fusion.1
  23.2 0.9 multiply_dynamic-update-slice_fusion
  24.1 0.8 fusion.30
  24.9 0.5 fusion.32
  25.3 0.9 broadcast_dynamic-update-slice_fusion
  26.3 8.6 %copy.31 = f32[10,120,1024]{2,0,1:T(8,128)} copy(f32[10,120,1024]{2,1,0:T(8,128)} %broadcast_dynamic-update-slice_fusion) | data formatting | bytes 9830400
  35.0 1.0 copy.33
  35.9 0.8 copy.32
  36.8 1.0 pad_maximum_fusion
  37.9 99.7 %while.26 = (s32[]{:T(128)}, f32[120,1024]{1,0:T(8,128)S(1)}, f32[120,1024]{1,0:T(8,128)S(1)}, bf16[2,120,1024]{2,1,0:T(8,128)(2,1)}, f32[2,120,1024]{2,1,0:T(8,...) while((s32[]{:T(128)}, f32[120,1024]{1,0:T(8,128)S(1)}, ...), condition=%wide.region_2.3_spmd.clone.clone.clone, body=%wide.region_0.2_spmd.sunk.clone.clone.clone.sunk | while | flops 1026297152 | bytes 74979888 | solution.py:105
  38.1 0.7 fusion.69
  38.8 0.6 fusion.70
  39.4 6.2 %and_select_fusion.3 = f32[120]{0:T(128)S(1)} fusion(pred[120]{0:T(512)(128)(4,1)S(1)} %get-tuple-element.900, pred[120]{0:T(512)(128)(4,1)S(1)} %get-tuple-element.901, pred[120]{0:T(512)(128)(4,1)S(1)} %get-tuple-element.902, pred[120]{0:T(512)(128)(4,1)S(1)} %get-tuple-element.903, pred[120]{0:T(512)(128)(4,1)S(1)} %get-tuple-element.904, ...), kind=kLoop, calls=%fused_computation.32.clone.1 | loop fusion | flops 3240 | bytes 1364 | tf_op jit(solution)/shard_map/while/body/eval_jaxpr/mul | solution.py:49
  45.5 3.3 %convert_bitcast_fusion.3 = bf16[9,120,1024]{2,1,0:T(8,128)(2,1)} fusion(bf16[9,120,142]{1,2,0:T(8,128)(2,1)} %get-tuple-element.896, bf16[2,142,1024]{2,1,0:T(8,128)(2,1)} %get-tuple-element.895, s32[]{:T(128)} %get-tuple-element.858), kind=kOutput, calls=%fused_computation.8.clone.1 | convolution fusion | flops 315187200 | bytes 2839040 | tf_op jit(solution)/shard_map/while/body/eval_jaxpr/bih,hc->bic/dot_general | solution.py:83
  48.8 3.0 copy.61
  51.8 0.6 pad.26.clone.2
  52.4 2.6 fusion.71
  55.0 4.4 %copy.62 = bf16[9,120,8,128]{3,2,1,0:T(8,128)(2,1)} copy(bf16[9,120,8,128]{1,3,2,0:T(8,128)(2,1)} %get-tuple-element.828) | data formatting | bytes 4423680 | tf_op jit(solution)/shard_map/while
  59.4 2.6 copy.63
  62.0 5.7 %fusion.72 = f32[9,120,8,128]{3,2,1,0:T(8,128)} fusion(bf16[9,120,8,128]{3,2,1,0:T(8,128)(2,1)} %copy.62, bf16[9,120,8,128]{3,2,1,0:T(8,128)(2,1)} %copy.63, bf16[9,256,128]{2,1,0:T(8,128)(2,1)} %get-tuple-element.897), kind=kOutput, calls=%fused_computation.4.clone.1 | convolution fusion | flops 575078400 | bytes 9437184 | tf_op jit(solution)/shard_map/while/body/eval_jaxpr/brjk,bkc->brjc/dot_general | solution.py:90
  67.7 5.5 %reshape.423 = f32[9,120,1024]{2,1,0:T(8,128)} reshape(f32[9,120,8,128]{3,2,1,0:T(8,128)} %fusion.72) | data formatting | bytes 8847360 | tf_op jit(solution)/shard_map/while/body/eval_jaxpr/reshape | solution.py:92
  73.3 13.1 %fusion.74 = bf16[120,1024]{1,0:T(8,128)(2,1)S(1)} fusion(f32[9,120,1024]{2,1,0:T(8,128)} %reshape.423, f32[10,120,1024]{2,0,1:T(8,128)} %get-tuple-element.894, f32[1,9,10]{2,0,1:T(1,128)S(1)} %constant_dynamic-slice_fusion.9, s32[10]{0:T(128)S(1)} %get-tuple-element.909, s32[9]{0:T(128)S(1)} %fusion.73), kind=kOutput, calls=%fused_computation.3.clone.1 | convolution fusion | flops 134799536 | bytes 9585076 | tf_op jit(solution)/shard_map/while/body/eval_jaxpr/bt,trc->brc/dot_general | solution.py:93
  86.4 0.2 select_add_fusion.3
  86.6 0.1 fusion.75
  86.7 0.9 copy-done.4
  87.7 0.2 copy-done.7
  87.8 0.7 fusion.69
  88.5 0.6 fusion.70
  89.1 6.2 %and_select_fusion.3 = f32[120]{0:T(128)S(1)} fusion(pred[120]{0:T(512)(128)(4,1)S(1)} %get-tuple-element.900, pred[120]{0:T(512)(128)(4,1)S(1)} %get-tuple-element.901, pred[120]{0:T(512)(128)(4,1)S(1)} %get-tuple-element.902, pred[120]{0:T(512)(128)(4,1)S(1)} %get-tuple-element.903, pred[120]{0:T(512)(128)(4,1)S(1)} %get-tuple-element.904, ...), kind=kLoop, calls=%fused_computation.32.clone.1 | loop fusion | flops 3240 | bytes 1364 | tf_op jit(solution)/shard_map/while/body/eval_jaxpr/mul | solution.py:49
  95.3 3.3 %convert_bitcast_fusion.3 = bf16[9,120,1024]{2,1,0:T(8,128)(2,1)} fusion(bf16[9,120,142]{1,2,0:T(8,128)(2,1)} %get-tuple-element.896, bf16[2,142,1024]{2,1,0:T(8,128)(2,1)} %get-tuple-element.895, s32[]{:T(128)} %get-tuple-element.858), kind=kOutput, calls=%fused_computation.8.clone.1 | convolution fusion | flops 315187200 | bytes 2839040 | tf_op jit(solution)/shard_map/while/body/eval_jaxpr/bih,hc->bic/dot_general | solution.py:83
  98.6 3.0 copy.61
  101.6 0.6 pad.26.clone.2
  102.1 2.6 fusion.71
  104.8 4.4 %copy.62 = bf16[9,120,8,128]{3,2,1,0:T(8,128)(2,1)} copy(bf16[9,120,8,128]{1,3,2,0:T(8,128)(2,1)} %get-tuple-element.828) | data formatting | bytes 4423680 | tf_op jit(solution)/shard_map/while
  109.1 2.6 copy.63
  111.7 5.7 %fusion.72 = f32[9,120,8,128]{3,2,1,0:T(8,128)} fusion(bf16[9,120,8,128]{3,2,1,0:T(8,128)(2,1)} %copy.62, bf16[9,120,8,128]{3,2,1,0:T(8,128)(2,1)} %copy.63, bf16[9,256,128]{2,1,0:T(8,128)(2,1)} %get-tuple-element.897), kind=kOutput, calls=%fused_computation.4.clone.1 | convolution fusion | flops 575078400 | bytes 9437184 | tf_op jit(solution)/shard_map/while/body/eval_jaxpr/brjk,bkc->brjc/dot_general | solution.py:90
  117.5 5.5 %reshape.423 = f32[9,120,1024]{2,1,0:T(8,128)} reshape(f32[9,120,8,128]{3,2,1,0:T(8,128)} %fusion.72) | data formatting | bytes 8847360 | tf_op jit(solution)/shard_map/while/body/eval_jaxpr/reshape | solution.py:92
  123.0 13.1 %fusion.74 = bf16[120,1024]{1,0:T(8,128)(2,1)S(1)} fusion(f32[9,120,1024]{2,1,0:T(8,128)} %reshape.423, f32[10,120,1024]{2,0,1:T(8,128)} %get-tuple-element.894, f32[1,9,10]{2,0,1:T(1,128)S(1)} %constant_dynamic-slice_fusion.9, s32[10]{0:T(128)S(1)} %get-tuple-element.909, s32[9]{0:T(128)S(1)} %fusion.73), kind=kOutput, calls=%fused_computation.3.clone.1 | convolution fusion | flops 134799536 | bytes 9585076 | tf_op jit(solution)/shard_map/while/body/eval_jaxpr/bt,trc->brc/dot_general | solution.py:93
  136.1 0.2 select_add_fusion.3
  136.3 0.1 fusion.75
  136.5 0.9 copy-done.4
  137.4 0.2 copy-done.7
  137.6 0.8 copy-done
  138.3 0.2 copy-done.1
  138.5 0.0 all-reduce.4.cloned.1.call-update
  138.5 0.0 reduce-scatter.3.cloned.1.call-start
  138.6 83.1 %all-reduce.4.cloned.1.call-done = (f32[120,1024]{1,0:T(8,128)}, f32[120,1024]{1,0:T(8,128)}) async-done(((f32[120,1024]{1,0:T(8,128)}, f32[120,1024]{1,0:T(8,128)}), (f32[120,1024]{1,0:T(8,128)}, f32[120,1024]{1,0:T(8,128)})) %all-reduce.4.cloned.1.call-update) | async-done | bytes 983056 | tf_op jit(solution)/shard_map/psum | solution.py:108
  221.7 1.2 add_divide_fusion
  223.0 3.0 fusion.42
  226.0 0.0 reduce-scatter.5.cloned.1.call-start
  226.1 0.7 reduce-scatter.5.cloned.1.call-update
  226.8 39.7 %reduce-scatter.3.cloned.1.call-done = f32[120,128]{1,0:T(8,128)} async-done(((f32[120,1024]{1,0:T(8,128)}), f32[120,128]{1,0:T(8,128)}) %reduce-scatter.3.cloned.1.call-update) | async-done | bytes 61456 | tf_op jit(solution)/shard_map/reduce_scatter | solution.py:116
  266.5 42.1 %reduce-scatter.5.cloned.1.call-done = f32[120,128]{1,0:T(8,128)} async-done(((f32[120,1024]{1,0:T(8,128)}), f32[120,128]{1,0:T(8,128)}) %reduce-scatter.5.cloned.1.call-update) | async-done | bytes 61456 | tf_op jit(solution)/shard_map/reduce_scatter | solution.py:117
  308.5 1.5 add_divide_fusion.1
  (72 shorter events, 0.3 us)
Async XLA Ops:
  6.5 17.5 %copy-start.9 = (bf16[9,2,23]{2,1,0:T(2,128)(2,1)S(1)}, bf16[9,2,23]{2,1,0:T(2,128)(2,1)}, u32[]{:S(2)}) copy-start(bf16[9,2,23]{2,1,0:T(2,128)(2,1)} %param.14) | copy-start | bytes 2488
  6.5 215.2 %all-reduce.4.cloned.1.call-start = ((), (), s32[]{:S(2)}) async-start(), calls=%async_computation.4 | async-start | bytes 1966080 | tf_op jit(solution)/shard_map/psum | solution.py:108
  7.4 29.3 %collective-permute-start = (bf16[2,11,1024]{2,1,0:T(8,128)(2,1)S(1)}, bf16[2,11,1024]{2,1,0:T(8,128)(2,1)S(1)}, u32[]{:S(2)}, u32[]{:S(2)}) collective-permute-start(bf16[2,11,1024]{2,1,0:T(8,128)(2,1)S(1)} %get-tuple-element.707), channel_id=1, source_target_pairs={{0,8},{8,16},{16,24},{24,32},{32,40},{40,48},{48,56},{56,64},{64,7... | collective-permute-start | bytes 135176 | tf_op jit(solution)/shard_map/ppermute | solution.py:18
  9.4 27.4 %collective-permute-start.1 = (bf16[2,11,1024]{2,1,0:T(8,128)(2,1)S(1)}, bf16[2,11,1024]{2,1,0:T(8,128)(2,1)S(1)}, u32[]{:S(2)}, u32[]{:S(2)}) collective-permute-start(bf16[2,11,1024]{2,1,0:T(8,128)(2,1)S(1)} %get-tuple-element.708), channel_id=1, source_target_pairs={{8,0},{16,8},{24,16},{32,24},{40,32},{48,40},{56,48},{64,56},{72,6... | collective-permute-start | bytes 135176 | tf_op jit(solution)/shard_map/ppermute | solution.py:20
  26.2 10.6 %copy-start.5 = (bf16[2,120,1024]{2,1,0:T(8,128)(2,1)S(1)}, bf16[2,120,1024]{2,1,0:T(8,128)(2,1)}, u32[]{:S(2)}) copy-start(bf16[2,120,1024]{2,1,0:T(8,128)(2,1)} %param.12) | copy-start | bytes 1474564
  26.2 11.6 %copy-start.8 = (f32[2,9,10]{2,0,1:T(2,128)S(1)}, f32[2,9,10]{2,0,1:T(2,128)}, u32[]{:S(2)}) copy-start(f32[2,9,10]{2,0,1:T(2,128)} %param.15) | copy-start | bytes 2164
  26.2 11.6 %copy-start.10 = (s32[10]{0:T(128)S(1)}, s32[10]{0:T(128)}, u32[]{:S(2)}) copy-start(s32[10]{0:T(128)} %constant.261.clone..sunk.4) | copy-start | bytes 124
  26.2 11.6 %copy-start.11 = (pred[120]{0:T(512)(128)(4,1)S(1)}, pred[120]{0:T(512)(128)(4,1)}, u32[]{:S(2)}) copy-start(pred[120]{0:T(512)(128)(4,1)} %constant.377) | copy-start | bytes 364
  26.2 11.6 %copy-start.12 = (pred[120]{0:T(512)(128)(4,1)S(1)}, pred[120]{0:T(512)(128)(4,1)}, u32[]{:S(2)}) copy-start(pred[120]{0:T(512)(128)(4,1)} %constant.378) | copy-start | bytes 364
  26.2 11.6 %copy-start.13 = (pred[120]{0:T(512)(128)(4,1)S(1)}, pred[120]{0:T(512)(128)(4,1)}, u32[]{:S(2)}) copy-start(pred[120]{0:T(512)(128)(4,1)} %constant.379) | copy-start | bytes 364
  26.3 11.5 %copy-start.14 = (pred[120]{0:T(512)(128)(4,1)S(1)}, pred[120]{0:T(512)(128)(4,1)}, u32[]{:S(2)}) copy-start(pred[120]{0:T(512)(128)(4,1)} %constant.380) | copy-start | bytes 364
  26.3 11.5 %copy-start.15 = (pred[120]{0:T(512)(128)(4,1)S(1)}, pred[120]{0:T(512)(128)(4,1)}, u32[]{:S(2)}) copy-start(pred[120]{0:T(512)(128)(4,1)} %constant.381) | copy-start | bytes 364
  26.3 11.5 %copy-start.16 = (pred[120]{0:T(512)(128)(4,1)S(1)}, pred[120]{0:T(512)(128)(4,1)}, u32[]{:S(2)}) copy-start(pred[120]{0:T(512)(128)(4,1)} %constant.382) | copy-start | bytes 364
  26.3 11.5 %copy-start.17 = (pred[120]{0:T(512)(128)(4,1)S(1)}, pred[120]{0:T(512)(128)(4,1)}, u32[]{:S(2)}) copy-start(pred[120]{0:T(512)(128)(4,1)} %constant.383) | copy-start | bytes 364
  26.3 11.5 %copy-start.18 = (s32[2,2]{1,0:T(2,128)S(1)}, s32[2,2]{1,0:T(2,128)}, u32[]{:S(2)}) copy-start(s32[2,2]{1,0:T(2,128)} %param.17) | copy-start | bytes 52
  26.3 11.5 %copy-start.19 = (s32[2,8]{1,0:T(2,128)S(1)}, s32[2,8]{1,0:T(2,128)}, u32[]{:S(2)}) copy-start(s32[2,8]{1,0:T(2,128)} %param.18) | copy-start | bytes 196
  26.3 11.5 %copy-start.20 = (s32[2,9]{1,0:T(2,128)S(1)}, s32[2,9]{1,0:T(2,128)}, u32[]{:S(2)}) copy-start(s32[2,9]{1,0:T(2,128)} %param.16) | copy-start | bytes 220
  73.2 13.1 %copy-start.2 = (bf16[2,120,1024]{2,1,0:T(8,128)(2,1)S(1)}, bf16[2,120,1024]{2,1,0:T(8,128)(2,1)}, u32[]{:S(2)}) copy-start(bf16[2,120,1024]{2,1,0:T(8,128)(2,1)} %get-tuple-element.891) | copy-start | bytes 1474564 | tf_op jit(solution)/shard_map/while
  73.3 13.3 %copy-start.3 = (f32[2,120,1024]{2,1,0:T(8,128)S(1)}, f32[2,120,1024]{2,1,0:T(8,128)}, u32[]{:S(2)}) copy-start(f32[2,120,1024]{2,1,0:T(8,128)} %get-tuple-element.862) | copy-start | bytes 2949124 | tf_op jit(solution)/shard_map/while
  73.3 13.4 %copy-start.6 = (bf16[2,120,1024]{2,1,0:T(8,128)(2,1)S(1)}, bf16[2,120,1024]{2,1,0:T(8,128)(2,1)}, u32[]{:S(2)}) copy-start(bf16[2,120,1024]{2,1,0:T(8,128)(2,1)} %get-tuple-element.861) | copy-start | bytes 1474564 | tf_op jit(solution)/shard_map/while
  86.7 1.0 copy-start.4
  86.7 1.1 copy-start.7
  123.0 13.1 %copy-start.2 = (bf16[2,120,1024]{2,1,0:T(8,128)(2,1)S(1)}, bf16[2,120,1024]{2,1,0:T(8,128)(2,1)}, u32[]{:S(2)}) copy-start(bf16[2,120,1024]{2,1,0:T(8,128)(2,1)} %get-tuple-element.891) | copy-start | bytes 1474564 | tf_op jit(solution)/shard_map/while
  123.0 13.3 %copy-start.3 = (f32[2,120,1024]{2,1,0:T(8,128)S(1)}, f32[2,120,1024]{2,1,0:T(8,128)}, u32[]{:S(2)}) copy-start(f32[2,120,1024]{2,1,0:T(8,128)} %get-tuple-element.862) | copy-start | bytes 2949124 | tf_op jit(solution)/shard_map/while
  123.0 13.4 %copy-start.6 = (bf16[2,120,1024]{2,1,0:T(8,128)(2,1)S(1)}, bf16[2,120,1024]{2,1,0:T(8,128)(2,1)}, u32[]{:S(2)}) copy-start(bf16[2,120,1024]{2,1,0:T(8,128)(2,1)} %get-tuple-element.861) | copy-start | bytes 1474564 | tf_op jit(solution)/shard_map/while
  136.4 1.0 copy-start.4
  136.5 1.1 copy-start.7
  137.6 0.8 copy-start
  137.6 1.0 copy-start.1
  138.5 127.9 %reduce-scatter.3.cloned.1.call-start = ((), (), s32[]{:S(2)}) async-start(), calls=%async_computation.2 | async-start | bytes 552960 | tf_op jit(solution)/shard_map/reduce_scatter | solution.py:116
  226.0 82.5 %reduce-scatter.5.cloned.1.call-start = ((), (), s32[]{:S(2)}) async-start(), calls=%async_computation.3 | async-start | bytes 552960 | tf_op jit(solution)/shard_map/reduce_scatter | solution.py:117
Sparse Core Ops, SparseCore 0:
  138.7 83.0 all-reduce.3
  226.2 40.2 reduce-scatter.2
  269.0 39.4 reduce-scatter.4
where the time goes:
time: 318 us; the launch traced here: 317 us
  waiting for transfers between devices  166 us (52%)
  local copies, waits for them, and re-layouts  60.6 us (19%)
  matrix products  45.4 us (14%)
  other arithmetic  22.4 us (7%)
  between operations  13.3 us (4%)
  starting transfers between devices  8.66 us (3%)
    psum x1, waiting for transfers between devices, body(): num_whole, den_whole = lax.psum((num_first, den_first), 'exp')  83.1 us
    reduce_scatter x1, waiting for transfers between devices, body(): lax.psum_scatter(den_final, 'exp', scatter_dimension=1, tiled=True)  42.1 us
    reduce_scatter x1, waiting for transfers between devices, body(): lax.psum_scatter(num_final, 'exp', scatter_dimension=1, tiled=True)  39.7 us
    dot_general x2, matrix products, first_pass(): jnp.einsum('bt,trc->brc', coef * term_active(degree), terms_field, precis...  26.1 us
    while x26, local copies, waits for them, and re-layouts  22.1 us
    unnamed x41, local copies, waits for them, and re-layouts  16.7 us
    mul x2, other arithmetic, pixel_weight(): return (covered * usable)[:, None] / var_field.astype(jnp.float32)  12.3 us
    dot_general x2, matrix products, first_pass(): jnp.einsum('brjk,bkc->brjc', windows, col_band, preferred_element_type=jn...  11.5 us
  transfers between devices with their start and end apart: 5, of which 3 were waited for; matrix products, arithmetic and copies ran while one was open for 6% of the time, Pallas kernels for 0%

commit v1 on v0

v1 whole, which is shorter than its diff:
```python
import functools

import jax
import jax.numpy as jnp
from jax import lax
from jax.experimental import pallas as pl
from jax.experimental.pallas import tpu as pltpu
from jax.sharding import PartitionSpec as P

MESH = pl.DeviceIdType.MESH
F32, BF16 = jnp.float32, jnp.bfloat16
TOP, BOT, KROWS = 128, 144, 160
HALO = 16
EXPS, ROWS, COLS, NB, KW = 2, 120, 1024, 9, 23
HALF = KW // 2
BLOCKS = 8
ORDERS = (0, 1, 1, 2, 2, 2, 3, 3, 3, 3)


def iota(shape, dim):
    return lax.broadcasted_iota(jnp.int32, shape, dim)


def kernel(
    n_sky, n_exp, coeffs, degrees, footprint, masks, taps, warped, variance, out,
    raw, halo, vraw, image, tapbuf, rowband, colband, gains, along, vsend, msend, vrecv, mrecv, weights,
    local_sems, halo_send, halo_recv, v_send, v_recv, m_send, m_recv,
):
    sky, me = lax.axis_index("sky"), lax.axis_index("exp")
    above, below = lax.rem(sky + n_sky - 1, n_sky), lax.rem(sky + 1, n_sky)
    peers = [lax.rem(me + t, n_exp) for t in range(n_exp)]

    own_copy = pltpu.make_async_copy(warped, raw, local_sems.at[0])
    var_copy = pltpu.make_async_copy(variance, vraw, local_sems.at[1])
    var_copy.start()
    own_copy.start()

    barrier = pltpu.get_barrier_semaphore()
    for t in range(1, n_exp):
        pl.semaphore_signal(barrier, inc=1, device_id=(sky, peers[t]), device_id_type=MESH)
    for row in (above, below):
        pl.semaphore_signal(barrier, inc=1, device_id=(row, me), device_id_type=MESH)

    tapbuf[...] = jnp.zeros_like(tapbuf)
    for b in range(NB):
        tapbuf[2 * b : 2 * b + 2, 0:KW] = taps[b].astype(F32)

    def band(row, k, valid):
        table = jnp.broadcast_to(tapbuf[row : row + 1, :], k.shape)
        picked = jnp.take_along_axis(table, jnp.clip(k, 0, 127), axis=1)
        return jnp.where(valid & (k >= 0) & (k < KW), picked, 0.0).astype(BF16)

    kappa, cols = iota((256, 128), 0), iota((256, 128), 1)
    k_col = kappa - cols - (64 - HALF)
    for b in range(NB):
        colband[b] = band(2 * b + 1, k_col, k_col == k_col)
    r_low, k_low = iota((128, 128), 0), iota((128, 128), 1)
    k_own = k_low - r_low + HALF
    valid_own = k_low < ROWS
    where_row = jnp.where(k_low < HALO, k_low - HALO, k_low + (ROWS - HALO))
    k_halo = where_row - r_low + HALF
    valid_halo = (k_low < 2 * HALO) & ((k_low >= HALO) | (sky > 0)) & ((k_low < HALO) | (sky < n_sky - 1))
    for b in range(NB):
        rowband[128 * b : 128 * b + 128, 0:128] = band(2 * b, k_own, valid_own)
        rowband[128 * b : 128 * b + 128, 128:KROWS] = band(2 * b, k_halo, valid_halo)[:, 0 : KROWS - 128]

    pl.semaphore_wait(barrier, n_exp - 1 + 2)

    down = pltpu.make_async_remote_copy(
        src_ref=warped.at[:, ROWS - HALO : ROWS, :], dst_ref=halo.at[0],
        send_sem=halo_send.at[0], recv_sem=halo_recv.at[0], device_id=(below, me), device_id_type=MESH,
    )
    up = pltpu.make_async_remote_copy(
        src_ref=warped.at[:, 0:HALO, :], dst_ref=halo.at[1],
        send_sem=halo_send.at[1], recv_sem=halo_recv.at[1], device_id=(above, me), device_id_type=MESH,
    )
    down.start()
    up.start()

    var_copy.wait()
    rows = iota((ROWS, 128), 0)
    word_at = (rows * 137) >> 11
    offset = 2 * (rows - 15 * word_at)
    for e in range(EXPS):
        word = jnp.zeros((ROWS, 128), jnp.int32)
        for i in range(ROWS // 15):
            word = jnp.where(word_at == i, masks[e, i], word)
        global_row = sky * ROWS + rows
        usable = (
            (((word >> offset) & 3) != 3)
            & (global_row >= footprint[e, 0])
            & (global_row < footprint[e, 1])
        )
        for t in range(n_exp):
            block = vraw[e, :, pl.ds(pl.multiple_of(peers[t] * 128, 128), 128)].astype(F32)
            masked = jnp.where(usable, block, 0.0).astype(BF16)
            if t == 0:
                vrecv[0, e] = masked
            else:
                vsend[t - 1, e] = masked

    v_copies, m_copies = [], []
    for t in range(1, n_exp):
        v_copies.append(pltpu.make_async_remote_copy(
            src_ref=vsend.at[t - 1], dst_ref=vrecv.at[t],
            send_sem=v_send.at[t], recv_sem=v_recv.at[t], device_id=(sky, peers[t]), device_id_type=MESH,
        ))
        m_copies.append(pltpu.make_async_remote_copy(
            src_ref=msend.at[t - 1], dst_ref=mrecv.at[t],
            send_sem=m_send.at[t], recv_sem=m_recv.at[t], device_id=(sky, peers[t]), device_id_type=MESH,
        ))
    for copy in v_copies:
        copy.start()

    u = (2.0 * (sky * ROWS + iota((128, 128), 0)).astype(F32) + 1.0) / (n_sky * ROWS) - 1.0

    @pl.loop(0, NB)
    def _(b):
        for e in range(EXPS):
            degree = degrees[e, b]
            c = [jnp.where(ORDERS[t] <= degree, coeffs[e, b, t], 0.0) for t in range(10)]
            span = slice(128 * e, 128 * e + 128)
            gains[b, 0, span, :] = ((c[6] * u + c[3]) * u + c[1]) * u + c[0]
            gains[b, 1, span, :] = (c[7] * u + c[4]) * u + c[2]
            gains[b, 2, span, :] = c[8] * u + c[5]

    own_copy.wait()
    for e in range(EXPS):
        image[e, :, 0:128] = jnp.zeros((KROWS, 128), BF16)
        image[e, :, 1024:1152] = jnp.zeros((KROWS, 128), BF16)
        image[e, 112:128, :] = jnp.zeros((16, 1152), BF16)
        image[e, 0:ROWS, 64:1088] = raw[e]
    down.wait_recv()
    up.wait_recv()
    for e in range(EXPS):
        image[e, TOP : TOP + HALO, 64:1088] = halo[0, e]
        image[e, BOT : BOT + HALO, 64:1088] = halo[1, e]

    for e in range(EXPS):
        @pl.loop(0, 9)
        def _(n):
            span = pl.ds(pl.multiple_of(n * 128, 128), 128)
            filtered = jnp.dot(rowband[...], image[e, :, span], preferred_element_type=F32).astype(BF16)
            for b in range(NB):
                along[b, 128 * e : 128 * e + 128, span] = filtered[128 * b : 128 * b + 128]

    def matched_block(j):
        col = pl.multiple_of(j * 128, 128)
        v = (2.0 * (j * 128 + iota((64, 128), 1)).astype(F32) + 1.0) / COLS - 1.0
        sums = [jnp.zeros((64, 128), F32) for _ in range(4)]
        for b in range(NB):
            filtered = jnp.dot(along[b, :, pl.ds(col, 256)], colband[b], preferred_element_type=F32)
            for part in range(4):
                e, span = part // 2, slice(64 * part, 64 * part + 64)
                cubic = jnp.where(degrees[e, b] >= 3, coeffs[e, b, 9], 0.0)
                field = ((cubic * v + gains[b, 2, span, :]) * v + gains[b, 1, span, :]) * v + gains[b, 0, span, :]
                sums[part] = sums[part] + field * filtered[span]
        return sums

    def put(ref, sums):
        for e in range(EXPS):
            ref[e, 0:64] = sums[2 * e].astype(BF16)
            ref[e, 64:ROWS] = sums[2 * e + 1][0 : ROWS - 64].astype(BF16)

    for t in range(1, n_exp):
        put(msend.at[t - 1], matched_block(peers[t]))
        m_copies[t - 1].start()
    put(mrecv.at[0], matched_block(peers[0]))

    halves = ((0, 64), (64, ROWS))
    den = [jnp.zeros((hi - lo, 128), F32) for lo, hi in halves]
    for t in range(n_exp):
        if t > 0:
            v_copies[t - 1].wait_recv()
        for i, (lo, hi) in enumerate(halves):
            for e in range(EXPS):
                var = vrecv[t, e, lo:hi].astype(F32)
                weight = jnp.where(var > 0.0, 1.0 / var, 0.0)
                weights[t, e, lo:hi] = weight
                den[i] = den[i] + weight
    num = [jnp.zeros((hi - lo, 128), F32) for lo, hi in halves]
    for t in range(n_exp):
        if t > 0:
            m_copies[t - 1].wait_recv()
        for i, (lo, hi) in enumerate(halves):
            for e in range(EXPS):
                num[i] = num[i] + weights[t, e, lo:hi] * mrecv[t, e, lo:hi].astype(F32)
    for i, (lo, hi) in enumerate(halves):
        first = num[i] / (1.0 + den[i])
        num_final = jnp.zeros((hi - lo, 128), F32)
        den_final = jnp.zeros((hi - lo, 128), F32)
        for t in range(n_exp):
            for e in range(EXPS):
                value = mrecv[t, e, lo:hi].astype(F32)
                weight = weights[t, e, lo:hi]
                excess = value - first
                robust = weight / (1.0 + excess * excess * weight * (1.0 / 9.0))
                num_final = num_final + robust * value
                den_final = den_final + robust
        out[lo:hi, :] = num_final / (1.0 + den_final)

    down.wait_send()
    up.wait_send()
    for copy in v_copies + m_copies:
        copy.wait_send()


def solution(mesh):
    n_sky, n_exp = mesh.shape["sky"], mesh.shape["exp"]

    def body(warped, variance, basis_taps, coeffs, degrees, footprint, masks):
        smem = pl.BlockSpec(memory_space=pltpu.SMEM)
        hbm = pl.BlockSpec(memory_space=pl.ANY)
        vmem = pl.BlockSpec(memory_space=pltpu.VMEM)
        dma = pltpu.SemaphoreType.DMA
        return pl.pallas_call(
            functools.partial(kernel, n_sky, n_exp),
            out_shape=jax.ShapeDtypeStruct((ROWS, 128), F32),
            in_specs=[smem, smem, smem, smem, vmem, hbm, hbm],
            out_specs=vmem,
            scratch_shapes=[
                pltpu.VMEM((EXPS, ROWS, COLS), BF16),
                pltpu.VMEM((2, EXPS, HALO, COLS), BF16),
                pltpu.VMEM((EXPS, ROWS, COLS), BF16),
                pltpu.VMEM((EXPS, KROWS, COLS + 128), BF16),
                pltpu.VMEM((24, 128), F32),
                pltpu.VMEM((NB * 128, KROWS), BF16),
                pltpu.VMEM((NB, 256, 128), BF16),
                pltpu.VMEM((NB, 3, 256, 128), F32),
                pltpu.VMEM((NB, 256, COLS + 128), BF16),
                pltpu.VMEM((n_exp - 1, EXPS, ROWS, 128), BF16),
                pltpu.VMEM((n_exp - 1, EXPS, ROWS, 128), BF16),
                pltpu.VMEM((n_exp, EXPS, ROWS, 128), BF16),
                pltpu.VMEM((n_exp, EXPS, ROWS, 128), BF16),
                pltpu.VMEM((n_exp, EXPS, ROWS, 128), F32),
                dma((2,)), dma((2,)), dma((2,)),
                dma((n_exp,)), dma((n_exp,)), dma((n_exp,)), dma((n_exp,)),
            ],
            compiler_params=pltpu.CompilerParams(
                collective_id=0, has_side_effects=True, vmem_limit_bytes=60 * 1024 * 1024
            ),
            name="coadd",
        )(coeffs, degrees, footprint, masks, basis_taps, warped, variance)

    in_specs = (
        P("exp", "sky", None),
        P("exp", "sky", None),
        P(),
        P("exp", None, None),
        P("exp", None),
        P("exp", None),
        P("exp", "sky"),
    )
    return jax.shard_map(body, mesh=mesh, in_specs=in_specs, out_specs=P("sky", "exp"), check_vma=False)
```

time: 318 us -> 32.6 us (0.10)
  the two profiles are of different devices: /device:TPU:64 before, /device:TPU:6 now
where the time goes in v1:
time: 32.6 us; the launch traced here: 32.4 us
  Pallas kernels  29.6 us (91%)
  local copies, waits for them, and re-layouts  2.76 us (8%)
    pallas_call x1, Pallas kernels, body(): pl.pallas_call(functools.partial(kernel, n_sky, n_exp), out_shape=jax.Sha...  29.6 us
    unnamed x2, local copies, waits for them, and re-layouts  2.76 us

profile of v1, /device:TPU:6, one launch (start us, length us, event | category | flops | bytes accessed | tf_op | source)
XLA Modules:
  0.0 32.4 jit_solution(12431052123465731426)
XLA Ops:
  0.0 1.3 %copy.8.coeffs = f32[2,9,10]{2,1,0:T(8,128)} copy(f32[2,9,10]{2,0,1:T(2,128)} %param.10) | data formatting | bytes 1440 | tf_op args[3]
  1.3 29.6 %coadd.1 = f32[120,128]{1,0:T(8,128)} custom-call(f32[2,9,10]{2,1,0:T(8,128)} %copy.8.coeffs, s32[2,9]{1,0:T(2,128)} %degrees.1, s32[2,2]{1,0:T(2,128)} %footprint.1, s32[2,8]{1,0:T(2,128)} %masks.1, bf16[9,2,23]{2,1,0:T(2,128)(2,1)} %taps.1, bf16[2,120,1024]{2,1,0:T(8,128)(2,1)} %warped.1, bf16[2,120,1024]{2,1,0:T(8,128)(2,1)} %variance.1), custom_call_target="tpu_custom_call" | custom-call | tf_op jit(solution)/shard_map/coadd/pallas_call | solution.py:216
  30.9 1.5 %copy.10 = f32[120,128]{1,0:T(8,128)} copy(f32[120,128]{1,0:T(8,128)} %coadd.1) | data formatting | bytes 122880

commit v2 on v1

v2 whole, which is shorter than its diff:
```python
import functools

import jax
import jax.numpy as jnp
from jax import lax
from jax.experimental import pallas as pl
from jax.experimental.pallas import tpu as pltpu
from jax.sharding import PartitionSpec as P

MESH = pl.DeviceIdType.MESH
F32, BF16 = jnp.float32, jnp.bfloat16
EXPS, ROWS, COLS, NB, KW = 2, 120, 1024, 9, 23
HALF = KW // 2
HALO = 16
TOP, BOT, KROWS = 128, 144, 160
PAD = 16
ORDERS = (0, 1, 1, 2, 2, 2, 3, 3, 3, 3)
STEP = 16.0 / COLS


def iota(shape, dim):
    return lax.broadcasted_iota(jnp.int32, shape, dim)


def kernel(
    n_sky, n_exp, coeffs_hbm, degrees_hbm, footprint_hbm, masks_hbm, taps_hbm, warped, variance, out,
    coeffs, degrees, footprint, masks, taps, raw, vraw, image, tapbuf, rowband, colband, gains, along,
    vsend, msend, vrecv, mrecv, weights,
    small_sems, local_sems, halo_send, halo_recv, v_send, v_recv, m_send, m_recv,
):
    sky, me = lax.axis_index("sky"), lax.axis_index("exp")
    not_first, not_last = sky > 0, sky < n_sky - 1
    peers = [lax.rem(me + t, n_exp) for t in range(n_exp)]

    barrier = pltpu.get_barrier_semaphore()

    @pl.when(not_last)
    def _():
        pl.semaphore_signal(barrier, inc=1, device_id=(sky + 1, me), device_id_type=MESH)

    @pl.when(not_first)
    def _():
        pl.semaphore_signal(barrier, inc=1, device_id=(sky - 1, me), device_id_type=MESH)

    for t in range(1, n_exp):
        pl.semaphore_signal(barrier, inc=1, device_id=(sky, peers[t]), device_id_type=MESH)

    small = [
        pltpu.make_async_copy(src, dst, small_sems.at[i])
        for i, (src, dst) in enumerate((
            (taps_hbm, taps), (masks_hbm, masks), (footprint_hbm, footprint), (coeffs_hbm, coeffs), (degrees_hbm, degrees),
        ))
    ]
    for copy in small:
        copy.start()
    var_copy = pltpu.make_async_copy(variance, vraw.at[:, 0:ROWS, :], local_sems.at[0])
    own_copy = pltpu.make_async_copy(warped, raw.at[:, 0:ROWS, :], local_sems.at[1])
    var_copy.start()
    own_copy.start()

    for e in range(EXPS):
        raw[e, ROWS:TOP, :] = jnp.zeros((TOP - ROWS, COLS), BF16)
        vraw[e, ROWS:128, :] = jnp.zeros((128 - ROWS, COLS), BF16)

    @pl.when(jnp.logical_not(not_first))
    def _():
        for e in range(EXPS):
            raw[e, TOP:BOT, :] = jnp.zeros((HALO, COLS), BF16)

    @pl.when(jnp.logical_not(not_last))
    def _():
        for e in range(EXPS):
            raw[e, BOT:KROWS, :] = jnp.zeros((HALO, COLS), BF16)

    tapbuf[...] = jnp.zeros_like(tapbuf)
    small[0].wait()
    for b in range(NB):
        tapbuf[2 * b : 2 * b + 2, 0:KW] = taps[b].astype(F32)

    def band(row, k, valid):
        table = jnp.broadcast_to(tapbuf[row : row + 1, :], k.shape)
        picked = jnp.take_along_axis(table, jnp.clip(k, 0, 127), axis=1)
        return jnp.where(valid & (k >= 0) & (k < KW), picked, 0.0).astype(BF16)

    low, lane = iota((128, 128), 0), iota((128, 128), 1)
    k_own = low - lane + HALF
    low_h, lane_h = iota((2 * HALO, 128), 0), iota((2 * HALO, 128), 1)
    k_halo = jnp.where(low_h < HALO, low_h - HALO, low_h + (ROWS - HALO)) - lane_h + HALF
    k_first = lane - low - (PAD - HALF)
    k_second = k_first + 128
    for b in range(NB):
        span = slice(128 * b, 128 * b + 128)
        rowband[0:TOP, span] = band(2 * b, k_own, low < ROWS)
        rowband[TOP:KROWS, span] = band(2 * b, k_halo, low_h >= 0)
        colband[b, :, 0:128] = band(2 * b + 1, k_first, low >= 0)
        colband[b, :, 128:KROWS] = band(2 * b + 1, k_second, low >= 0)[:, 0 : KROWS - 128]

    n_neighbours = not_first.astype(jnp.int32) + not_last.astype(jnp.int32)
    pl.semaphore_wait(barrier, n_exp - 1 + n_neighbours)

    down = pltpu.make_async_remote_copy(
        src_ref=warped.at[:, ROWS - HALO : ROWS, :], dst_ref=raw.at[:, TOP:BOT, :],
        send_sem=halo_send.at[0], recv_sem=halo_recv.at[0], device_id=(sky + 1, me), device_id_type=MESH,
    )
    up = pltpu.make_async_remote_copy(
        src_ref=warped.at[:, 0:HALO, :], dst_ref=raw.at[:, BOT:KROWS, :],
        send_sem=halo_send.at[1], recv_sem=halo_recv.at[1], device_id=(sky - 1, me), device_id_type=MESH,
    )

    @pl.when(not_last)
    def _():
        down.start()

    @pl.when(not_first)
    def _():
        up.start()

    small[1].wait()
    small[2].wait()
    var_copy.wait()
    rows = iota((8, 128), 1)
    word_at = (rows * 137) >> 11
    offset = 2 * (rows - 15 * word_at)
    for e in range(EXPS):
        word = jnp.zeros((8, 128), jnp.int32)
        for i in range(ROWS // 15):
            word = jnp.where(word_at == i, masks[e, i], word)
        global_row = sky * ROWS + rows
        usable = (
            (((word >> offset) & 3) != 3)
            & (global_row >= footprint[e, 0])
            & (global_row < footprint[e, 1])
            & (rows < ROWS)
        )
        keep = jnp.broadcast_to(usable.astype(F32)[0:1], (128, 128))
        for t in range(n_exp):
            block = vraw[e, :, pl.ds(pl.multiple_of(peers[t] * 128, 128), 128)].astype(F32).T
            masked = (block * keep).astype(BF16)
            if t == 0:
                vrecv[0, e] = masked
            else:
                vsend[t - 1, e] = masked

    v_copies, m_copies = [], []
    for t in range(1, n_exp):
        v_copies.append(pltpu.make_async_remote_copy(
            src_ref=vsend.at[t - 1], dst_ref=vrecv.at[t],
            send_sem=v_send.at[t], recv_sem=v_recv.at[t], device_id=(sky, peers[t]), device_id_type=MESH,
        ))
        m_copies.append(pltpu.make_async_remote_copy(
            src_ref=msend.at[t - 1], dst_ref=mrecv.at[t],
            send_sem=m_send.at[t], recv_sem=m_recv.at[t], device_id=(sky, peers[t]), device_id_type=MESH,
        ))
    for copy in v_copies:
        copy.start()

    small[3].wait()
    small[4].wait()
    u = (2.0 * (sky * ROWS + rows).astype(F32) + 1.0) / (n_sky * ROWS) - 1.0
    for b in range(NB):
        for e in range(EXPS):
            degree = degrees[e, b]
            c = [jnp.where(ORDERS[t] <= degree, coeffs[b, e, t], 0.0) for t in range(10)]
            gains[b, e, 0] = ((c[6] * u + c[3]) * u + c[1]) * u + c[0]
            gains[b, e, 1] = (c[7] * u + c[4]) * u + c[2]
            gains[b, e, 2] = c[8] * u + c[5]
            gains[b, e, 3] = jnp.full((8, 128), c[9], F32)

    for b in range(NB):
        along[b, 0:PAD, :] = jnp.zeros((PAD, 256), BF16)
        along[b, PAD + COLS : COLS + 2 * PAD, :] = jnp.zeros((PAD, 256), BF16)
    own_copy.wait()
    for e in range(EXPS):
        for i in range(COLS // 128):
            span = slice(128 * i, 128 * i + 128)
            image[e, span, 0:TOP] = raw[e, 0:TOP, span].astype(F32).T.astype(BF16)

    @pl.when(not_first)
    def _():
        down.wait_recv()

    @pl.when(not_last)
    def _():
        up.wait_recv()

    for e in range(EXPS):
        for i in range(COLS // 128):
            span = slice(128 * i, 128 * i + 128)
            image[e, span, TOP:KROWS] = raw[e, TOP:KROWS, span].astype(F32).T.astype(BF16)

    for e in range(EXPS):
        lanes = slice(128 * e, 128 * e + 128)

        @pl.loop(0, 4)
        def _(n):
            tile = rowband[:, pl.ds(pl.multiple_of(n * 256, 256), 256)]
            filtered = jnp.dot(image[e], tile, preferred_element_type=F32).astype(BF16)
            along[2 * n, PAD : PAD + COLS, lanes] = filtered[:, 0:128]
            along[2 * n + 1, PAD : PAD + COLS, lanes] = filtered[:, 128:256]

        filtered = jnp.dot(image[e], rowband[:, 1024:1152], preferred_element_type=F32).astype(BF16)
        along[8, PAD : PAD + COLS, lanes] = filtered

    def put_matched(ref, j):
        start = pl.multiple_of(j * 128, 128)
        v = (2.0 * (j * 128 + iota((8, 128), 0)).astype(F32) + 1.0) / COLS - 1.0
        first_arg = 2.0 * v + STEP
        second_arg = 3.0 * v * v + 3.0 * STEP * v + STEP * STEP
        third_arg = 3.0 * (v + STEP)
        sums = [[jnp.zeros((8, 128), F32) for _ in range(16)] for _ in range(EXPS)]
        for b in range(NB):
            window = along[b, pl.ds(start, KROWS), :]
            filtered = jnp.dot(colband[b], window, preferred_element_type=F32)
            for e in range(EXPS):
                g0, g1, g2, g3 = (gains[b, e, q] for q in range(4))
                field = ((g3 * v + g2) * v + g1) * v + g0
                d1 = (g1 + g2 * first_arg + g3 * second_arg) * STEP
                d2 = (g2 + g3 * third_arg) * (2.0 * STEP * STEP)
                d3 = g3 * (6.0 * STEP * STEP * STEP)
                for i in range(16):
                    part = filtered[8 * i : 8 * i + 8, 128 * e : 128 * e + 128]
                    sums[e][i] = sums[e][i] + field * part
                    if i < 15:
                        field = field + d1
                    if i < 14:
                        d1 = d1 + d2
                    if i < 13:
                        d2 = d2 + d3
        for e in range(EXPS):
            ref[e] = jnp.concatenate(sums[e], axis=0).astype(BF16)

    for t in range(1, n_exp):
        put_matched(msend.at[t - 1], peers[t])
        m_copies[t - 1].start()
    put_matched(mrecv.at[0], peers[0])

    halves = ((0, 64), (64, 128))
    zero = jnp.zeros((64, 128), F32)
    den = [zero, zero]
    for t in range(n_exp):
        if t > 0:
            v_copies[t - 1].wait_recv()
        for i, (lo, hi) in enumerate(halves):
            for e in range(EXPS):
                var = vrecv[t, e, lo:hi].astype(F32)
                weight = jnp.where(var > 0.0, 1.0 / var, 0.0)
                weights[t, e, lo:hi] = weight
                den[i] = den[i] + weight
    num = [zero, zero]
    for t in range(n_exp):
        if t > 0:
            m_copies[t - 1].wait_recv()
        for i, (lo, hi) in enumerate(halves):
            for e in range(EXPS):
                num[i] = num[i] + weights[t, e, lo:hi] * mrecv[t, e, lo:hi].astype(F32)
    finals = []
    for i, (lo, hi) in enumerate(halves):
        first = num[i] / (1.0 + den[i])
        num_final, den_final = zero, zero
        for t in range(n_exp):
            for e in range(EXPS):
                value = mrecv[t, e, lo:hi].astype(F32)
                weight = weights[t, e, lo:hi]
                excess = value - first
                robust = weight / (1.0 + excess * excess * weight * (1.0 / 9.0))
                num_final = num_final + robust * value
                den_final = den_final + robust
        finals.append(num_final / (1.0 + den_final))
    out[...] = jnp.concatenate(finals, axis=0).T[0:ROWS, :]

    @pl.when(not_last)
    def _():
        down.wait_send()

    @pl.when(not_first)
    def _():
        up.wait_send()

    for copy in v_copies + m_copies:
        copy.wait_send()


def solution(mesh):
    n_sky, n_exp = mesh.shape["sky"], mesh.shape["exp"]

    def body(warped, variance, basis_taps, coeffs, degrees, footprint, masks):
        hbm = pl.BlockSpec(memory_space=pl.ANY)
        vmem = pl.BlockSpec(memory_space=pltpu.VMEM)
        dma = pltpu.SemaphoreType.DMA
        return pl.pallas_call(
            functools.partial(kernel, n_sky, n_exp),
            out_shape=jax.ShapeDtypeStruct((ROWS, 128), F32),
            in_specs=[hbm] * 7,
            out_specs=vmem,
            scratch_shapes=[
                pltpu.SMEM((NB, EXPS, 10), F32),
                pltpu.SMEM((EXPS, NB), jnp.int32),
                pltpu.SMEM((EXPS, 2), jnp.int32),
                pltpu.SMEM((EXPS, 8), jnp.int32),
                pltpu.VMEM((NB, 2, KW), BF16),
                pltpu.VMEM((EXPS, KROWS, COLS), BF16),
                pltpu.VMEM((EXPS, 128, COLS), BF16),
                pltpu.VMEM((EXPS, COLS, KROWS), BF16),
                pltpu.VMEM((24, 128), F32),
                pltpu.VMEM((KROWS, NB * 128), BF16),
                pltpu.VMEM((NB, 128, KROWS), BF16),
                pltpu.VMEM((NB, EXPS, 4, 8, 128), F32),
                pltpu.VMEM((NB, COLS + 2 * PAD, 256), BF16),
                pltpu.VMEM((n_exp - 1, EXPS, 128, 128), BF16),
                pltpu.VMEM((n_exp - 1, EXPS, 128, 128), BF16),
                pltpu.VMEM((n_exp, EXPS, 128, 128), BF16),
                pltpu.VMEM((n_exp, EXPS, 128, 128), BF16),
                pltpu.VMEM((n_exp, EXPS, 128, 128), F32),
                dma((5,)), dma((2,)), dma((2,)), dma((2,)),
                dma((n_exp,)), dma((n_exp,)), dma((n_exp,)), dma((n_exp,)),
            ],
            compiler_params=pltpu.CompilerParams(
                collective_id=0, has_side_effects=True, vmem_limit_bytes=60 * 1024 * 1024
            ),
            name="coadd",
        )(coeffs.transpose(1, 0, 2), degrees, footprint, masks, basis_taps, warped, variance)

    in_specs = (
        P("exp", "sky", None),
        P("exp", "sky", None),
        P(),
        P("exp", None, None),
        P("exp", None),
        P("exp", None),
        P("exp", "sky"),
    )
    return jax.shard_map(body, mesh=mesh, in_specs=in_specs, out_specs=P("sky", "exp"), check_vma=False)
```

time: 32.6 us -> 23.9 us (0.73)
  the two profiles are of different devices: /device:TPU:6 before, /device:TPU:95 now
where the time goes in v2:
time: 23.9 us; the launch traced here: 23.8 us
  Pallas kernels  22.3 us (93%)
  local copies, waits for them, and re-layouts  1.46 us (6%)
    pallas_call x1, Pallas kernels, body(): pl.pallas_call(functools.partial(kernel, n_sky, n_exp), out_shape=jax.Sha...  22.3 us
    unnamed x1, local copies, waits for them, and re-layouts  1.46 us

profile of v2, /device:TPU:95, one launch (start us, length us, event | category | flops | bytes accessed | tf_op | source)
XLA Modules:
  0.0 23.8 jit_solution(11348297540809925751)
XLA Ops:
  0.0 22.3 %coadd.1 = f32[120,128]{1,0:T(8,128)} custom-call(f32[9,2,10]{2,1,0:T(2,128)} %bitcast.1, s32[2,9]{1,0:T(2,128)} %degrees_hbm.1, s32[2,2]{1,0:T(2,128)} %footprint_hbm.1, s32[2,8]{1,0:T(2,128)} %masks_hbm.1, bf16[9,2,23]{2,1,0:T(2,128)(2,1)} %taps_hbm.1, bf16[2,120,1024]{2,1,0:T(8,128)(2,1)} %warped.1, bf16[2,120,1024]{2,1,0:T(8,128)(2,1)} %variance.1), custom_call_target="tpu_custom_call" | custom-call | tf_op jit(solution)/shard_map/coadd/pallas_call | solution.py:290
  22.3 1.5 %copy.9 = f32[120,128]{1,0:T(8,128)} copy(f32[120,128]{1,0:T(8,128)} %coadd.1) | data formatting | bytes 122880

commit v3 on v2

v3 whole, which is shorter than its diff:
```python
import functools

import jax
import jax.numpy as jnp
from jax import lax
from jax.experimental import pallas as pl
from jax.experimental.pallas import tpu as pltpu
from jax.sharding import PartitionSpec as P

MESH = pl.DeviceIdType.MESH
F32, BF16 = jnp.float32, jnp.bfloat16
EXPS, ROWS, COLS, NB, KW = 2, 120, 1024, 9, 23
HALF = KW // 2
HALO = 16
LO, HI = 16, 104
INNER = HI - LO
EDGE = ROWS - INNER
EROWS = 96
PAD = 16
WINDOW = 160
ORDERS = (0, 1, 1, 2, 2, 2, 3, 3, 3, 3)
STEP = 16.0 / COLS


def iota(shape, dim):
    return lax.broadcasted_iota(jnp.int32, shape, dim)


def kernel(
    n_sky, n_exp, coeffs_hbm, degrees_hbm, footprint_hbm, masks_hbm, taps_hbm, warped, variance, out,
    coeffs, degrees, footprint, masks, taps, own, halo, vraw, image, edge_image, tapbuf, rowband, colband,
    edge_rowband, edge_colband, gains, edge_gains, along, edge_along,
    vsend, msend, esend, vrecv, mrecv, erecv, weights,
    small_sems, local_sems, halo_send, halo_recv, v_send, v_recv, m_send, m_recv, e_send, e_recv,
):
    sky, me = lax.axis_index("sky"), lax.axis_index("exp")
    not_first, not_last = sky > 0, sky < n_sky - 1
    peers = [lax.rem(me + t, n_exp) for t in range(n_exp)]

    barrier = pltpu.get_barrier_semaphore()

    @pl.when(not_last)
    def _():
        pl.semaphore_signal(barrier, inc=1, device_id=(sky + 1, me), device_id_type=MESH)

    @pl.when(not_first)
    def _():
        pl.semaphore_signal(barrier, inc=1, device_id=(sky - 1, me), device_id_type=MESH)

    for t in range(1, n_exp):
        pl.semaphore_signal(barrier, inc=1, device_id=(sky, peers[t]), device_id_type=MESH)

    small = [
        pltpu.make_async_copy(src, dst, small_sems.at[i])
        for i, (src, dst) in enumerate((
            (taps_hbm, taps), (masks_hbm, masks), (footprint_hbm, footprint), (coeffs_hbm, coeffs), (degrees_hbm, degrees),
        ))
    ]
    for copy in small:
        copy.start()
    var_copy = pltpu.make_async_copy(variance, vraw, local_sems.at[0])
    own_copy = pltpu.make_async_copy(warped, own, local_sems.at[1])
    var_copy.start()
    own_copy.start()

    @pl.when(jnp.logical_not(not_first))
    def _():
        halo[0] = jnp.zeros((EXPS, HALO, COLS), BF16)

    @pl.when(jnp.logical_not(not_last))
    def _():
        halo[1] = jnp.zeros((EXPS, HALO, COLS), BF16)

    tapbuf[...] = jnp.zeros_like(tapbuf)
    small[0].wait()
    for b in range(NB):
        tapbuf[2 * b : 2 * b + 2, 0:KW] = taps[b].astype(F32)

    def band(row, k):
        table = jnp.broadcast_to(tapbuf[row : row + 1, :], k.shape)
        picked = jnp.take_along_axis(table, jnp.clip(k, 0, 127), axis=1)
        return jnp.where((k >= 0) & (k < KW), picked, 0.0).astype(BF16)

    low, lane = iota((128, 128), 0), iota((128, 128), 1)
    k_row = jnp.where(low < ROWS, low - lane + HALF, -1)
    k_first = lane - low - (PAD - HALF)
    k_second = k_first + 128
    for b in range(NB):
        rowband[:, 128 * b : 128 * b + 128] = band(2 * b, k_row)
        colband[b, :, 0:128] = band(2 * b + 1, k_first)
        colband[b, :, 128:WINDOW] = band(2 * b + 1, k_second)[:, 0 : WINDOW - 128]

    small[1].wait()
    small[2].wait()
    var_copy.wait()
    rows = iota((ROWS, 128), 0)
    word_at = (rows * 137) >> 11
    offset = 2 * (rows - 15 * word_at)
    global_row = sky * ROWS + rows
    for e in range(EXPS):
        word = jnp.zeros((ROWS, 128), jnp.int32)
        for i in range(ROWS // 15):
            word = jnp.where(word_at == i, masks[e, i], word)
        usable = (
            (((word >> offset) & 3) != 3)
            & (global_row >= footprint[e, 0])
            & (global_row < footprint[e, 1])
        )
        for t in range(n_exp):
            block = vraw[e, :, pl.ds(pl.multiple_of(peers[t] * 128, 128), 128)].astype(F32)
            masked = jnp.where(usable, block, 0.0).astype(BF16)
            if t == 0:
                vrecv[0, e] = masked
            else:
                vsend[t - 1, e] = masked

    n_neighbours = not_first.astype(jnp.int32) + not_last.astype(jnp.int32)
    pl.semaphore_wait(barrier, n_exp - 1 + n_neighbours)

    down = pltpu.make_async_remote_copy(
        src_ref=warped.at[:, ROWS - HALO : ROWS, :], dst_ref=halo.at[0],
        send_sem=halo_send.at[0], recv_sem=halo_recv.at[0], device_id=(sky + 1, me), device_id_type=MESH,
    )
    up = pltpu.make_async_remote_copy(
        src_ref=warped.at[:, 0:HALO, :], dst_ref=halo.at[1],
        send_sem=halo_send.at[1], recv_sem=halo_recv.at[1], device_id=(sky - 1, me), device_id_type=MESH,
    )

    @pl.when(not_last)
    def _():
        down.start()

    @pl.when(not_first)
    def _():
        up.start()

    def to_peer(src, dst, send_sems, recv_sems, t):
        return pltpu.make_async_remote_copy(
            src_ref=src.at[t - 1], dst_ref=dst.at[t],
            send_sem=send_sems.at[t], recv_sem=recv_sems.at[t], device_id=(sky, peers[t]), device_id_type=MESH,
        )

    v_copies = [to_peer(vsend, vrecv, v_send, v_recv, t) for t in range(1, n_exp)]
    m_copies = [to_peer(msend, mrecv, m_send, m_recv, t) for t in range(1, n_exp)]
    e_copies = [to_peer(esend, erecv, e_send, e_recv, t) for t in range(1, n_exp)]
    for copy in v_copies:
        copy.start()

    small[3].wait()
    small[4].wait()

    def position(row):
        return (2.0 * (sky * ROWS + row).astype(F32) + 1.0) / (n_sky * ROWS) - 1.0

    def coefficients(b, e):
        degree = degrees[e, b]
        return [jnp.where(ORDERS[t] <= degree, coeffs[b, e, t], 0.0) for t in range(10)]

    def cubic(c, u):
        return ((c[6] * u + c[3]) * u + c[1]) * u + c[0], (c[7] * u + c[4]) * u + c[2], c[8] * u + c[5]

    u_lane = position(iota((8, 128), 1))
    i_edge = iota((EDGE, 128), 0)
    u_edge = position(jnp.where(i_edge < LO, i_edge, i_edge + INNER))
    for b in range(NB):
        for e in range(EXPS):
            c = coefficients(b, e)
            gains[b, e, 0], gains[b, e, 1], gains[b, e, 2] = cubic(c, u_lane)
            gains[b, e, 3] = jnp.full((8, 128), c[9], F32)

    for b in range(NB):
        along[b, 0:PAD, :] = jnp.zeros((PAD, 256), BF16)
        along[b, PAD + COLS : COLS + 2 * PAD, :] = jnp.zeros((PAD, 256), BF16)
    own_copy.wait()
    for e in range(EXPS):
        for i in range(COLS // 128):
            span = slice(128 * i, 128 * i + 128)
            block = jnp.concatenate([own[e, :, span].astype(F32), jnp.zeros((128 - ROWS, 128), F32)], axis=0)
            image[e, span, :] = block.T.astype(BF16)

    for e in range(EXPS):
        lanes = slice(128 * e, 128 * e + 128)

        @pl.loop(0, 4)
        def _(n):
            tile = rowband[:, pl.ds(pl.multiple_of(n * 256, 256), 256)]
            filtered = jnp.dot(image[e], tile, preferred_element_type=F32).astype(BF16)
            along[2 * n, PAD : PAD + COLS, lanes] = filtered[:, 0:128]
            along[2 * n + 1, PAD : PAD + COLS, lanes] = filtered[:, 128:256]

        filtered = jnp.dot(image[e], rowband[:, 1024:1152], preferred_element_type=F32).astype(BF16)
        along[8, PAD : PAD + COLS, lanes] = filtered

    def put_interior(ref, j):
        start = pl.multiple_of(j * 128, 128)
        v = (2.0 * (j * 128 + iota((8, 128), 0)).astype(F32) + 1.0) / COLS - 1.0
        first_arg = 2.0 * v + STEP
        second_arg = 3.0 * v * v + 3.0 * STEP * v + STEP * STEP
        third_arg = 3.0 * (v + STEP)
        sums = [[jnp.zeros((8, 128), F32) for _ in range(16)] for _ in range(EXPS)]
        for b in range(NB):
            window = along[b, pl.ds(start, WINDOW), :]
            filtered = jnp.dot(colband[b], window, preferred_element_type=F32)
            for e in range(EXPS):
                g0, g1, g2, g3 = (gains[b, e, q] for q in range(4))
                field = ((g3 * v + g2) * v + g1) * v + g0
                d1 = (g1 + g2 * first_arg + g3 * second_arg) * STEP
                d2 = (g2 + g3 * third_arg) * (2.0 * STEP * STEP)
                d3 = g3 * (6.0 * STEP * STEP * STEP)
                for i in range(16):
                    part = filtered[8 * i : 8 * i + 8, 128 * e : 128 * e + 128]
                    sums[e][i] = sums[e][i] + field * part
                    if i < 15:
                        field = field + d1
                    if i < 14:
                        d1 = d1 + d2
                    if i < 13:
                        d2 = d2 + d3
        for e in range(EXPS):
            ref[e] = jnp.concatenate(sums[e], axis=0).T[LO:HI].astype(BF16)

    for t in range(1, n_exp):
        put_interior(msend.at[t - 1], peers[t])
        m_copies[t - 1].start()
    put_interior(mrecv.at[0], peers[0])

    i_band, kappa = iota((EDGE, 128), 0), iota((EDGE, 128), 1)
    k_edge = (
        jnp.where(kappa < 48, kappa - HALO, kappa + 40) - jnp.where(i_band < LO, i_band, i_band + INNER) + HALF
    )
    k_edge = jnp.where(kappa < EROWS, k_edge, -1)
    kappa_col, col = iota((256, 128), 0), iota((256, 128), 1)
    k_edge_col = kappa_col - col - (64 - HALF)
    for b in range(NB):
        edge_rowband[EDGE * b : EDGE * b + EDGE, :] = band(2 * b, k_edge)[:, 0:EROWS]
        edge_colband[b] = band(2 * b + 1, k_edge_col)
        for e in range(EXPS):
            g = cubic(coefficients(b, e), u_edge)
            for q in range(3):
                edge_gains[b, q, EDGE * e : EDGE * e + EDGE, :] = g[q]
    for e in range(EXPS):
        edge_image[e, :, 0:128] = jnp.zeros((EROWS, 128), BF16)
        edge_image[e, :, 1024:1152] = jnp.zeros((EROWS, 128), BF16)
        edge_image[e, 16:48, 64:1088] = own[e, 0:32]
        edge_image[e, 48:80, 64:1088] = own[e, 88:120]

    @pl.when(not_first)
    def _():
        down.wait_recv()

    @pl.when(not_last)
    def _():
        up.wait_recv()

    for e in range(EXPS):
        edge_image[e, 0:16, 64:1088] = halo[0, e]
        edge_image[e, 80:96, 64:1088] = halo[1, e]

    for e in range(EXPS):
        for n in range(5):
            span = slice(256 * n, min(256 * n + 256, COLS + 128))
            filtered = jnp.dot(edge_rowband[...], edge_image[e, :, span], preferred_element_type=F32).astype(BF16)
            for b in range(NB):
                edge_along[b, EDGE * e : EDGE * e + EDGE, span] = filtered[EDGE * b : EDGE * b + EDGE]

    def put_edges(group):
        starts = [pl.multiple_of(peers[t] * 128, 128) for t in group]
        vs = [(2.0 * (peers[t] * 128 + iota((EDGE, 128), 1)).astype(F32) + 1.0) / COLS - 1.0 for t in group]
        sums = [[jnp.zeros((EDGE, 128), F32) for _ in range(EXPS)] for _ in group]
        for b in range(NB):
            windows = jnp.concatenate([edge_along[b, :, pl.ds(s, 256)] for s in starts], axis=0)
            filtered = jnp.dot(windows, edge_colband[b], preferred_element_type=F32)
            for e in range(EXPS):
                g3 = jnp.where(degrees[e, b] >= 3, coeffs[b, e, 9], 0.0)
                g0, g1, g2 = (edge_gains[b, q, EDGE * e : EDGE * e + EDGE, :] for q in range(3))
                for i, v in enumerate(vs):
                    part = filtered[2 * EDGE * i + EDGE * e : 2 * EDGE * i + EDGE * e + EDGE]
                    sums[i][e] = sums[i][e] + (((g3 * v + g2) * v + g1) * v + g0) * part
        for i, t in enumerate(group):
            ref = erecv.at[0] if t == 0 else esend.at[t - 1]
            for e in range(EXPS):
                ref[e] = sums[i][e].astype(BF16)
            if t > 0:
                e_copies[t - 1].start()

    put_edges((1, 2, 3, 4))
    put_edges((5, 6, 7, 0))

    inner_chunks = ((0, 48), (48, INNER))
    for t in range(n_exp):
        if t > 0:
            v_copies[t - 1].wait_recv()
        for e in range(EXPS):
            for lo, hi in ((0, LO), (LO, 64), (64, HI), (HI, ROWS)):
                var = vrecv[t, e, lo:hi].astype(F32)
                weights[t, e, lo:hi] = jnp.where(var > 0.0, 1.0 / var, 0.0)

    def coadd(values, weight_of, shape):
        num, den = jnp.zeros(shape, F32), jnp.zeros(shape, F32)
        for t in range(n_exp):
            for e in range(EXPS):
                weight = weight_of(t, e)
                num = num + weight * values(t, e)
                den = den + weight
        first = num / (1.0 + den)
        num, den = jnp.zeros(shape, F32), jnp.zeros(shape, F32)
        for t in range(n_exp):
            for e in range(EXPS):
                value, weight = values(t, e), weight_of(t, e)
                excess = value - first
                robust = weight / (1.0 + excess * excess * weight * (1.0 / 9.0))
                num = num + robust * value
                den = den + robust
        return num / (1.0 + den)

    for copy in m_copies:
        copy.wait_recv()
    for lo, hi in inner_chunks:
        out[LO + lo : LO + hi, :] = coadd(
            lambda t, e: mrecv[t, e, lo:hi].astype(F32), lambda t, e: weights[t, e, LO + lo : LO + hi], (hi - lo, 128)
        )
    for copy in e_copies:
        copy.wait_recv()
    edges = coadd(
        lambda t, e: erecv[t, e].astype(F32),
        lambda t, e: jnp.concatenate([weights[t, e, 0:LO], weights[t, e, HI:ROWS]], axis=0),
        (EDGE, 128),
    )
    out[0:LO, :] = edges[0:LO]
    out[HI:ROWS, :] = edges[LO:EDGE]

    @pl.when(not_last)
    def _():
        down.wait_send()

    @pl.when(not_first)
    def _():
        up.wait_send()

    for copy in v_copies + m_copies + e_copies:
        copy.wait_send()


def solution(mesh):
    n_sky, n_exp = mesh.shape["sky"], mesh.shape["exp"]

    def body(warped, variance, basis_taps, coeffs, degrees, footprint, masks):
        hbm = pl.BlockSpec(memory_space=pl.ANY)
        vmem = pl.BlockSpec(memory_space=pltpu.VMEM)
        dma = pltpu.SemaphoreType.DMA
        return pl.pallas_call(
            functools.partial(kernel, n_sky, n_exp),
            out_shape=jax.ShapeDtypeStruct((ROWS, 128), F32),
            in_specs=[hbm] * 7,
            out_specs=vmem,
            scratch_shapes=[
                pltpu.SMEM((NB, EXPS, 10), F32),
                pltpu.SMEM((EXPS, NB), jnp.int32),
                pltpu.SMEM((EXPS, 2), jnp.int32),
                pltpu.SMEM((EXPS, 8), jnp.int32),
                pltpu.VMEM((NB, 2, KW), BF16),
                pltpu.VMEM((EXPS, ROWS, COLS), BF16),
                pltpu.VMEM((2, EXPS, HALO, COLS), BF16),
                pltpu.VMEM((EXPS, ROWS, COLS), BF16),
                pltpu.VMEM((EXPS, COLS, 128), BF16),
                pltpu.VMEM((EXPS, EROWS, COLS + 128), BF16),
                pltpu.VMEM((24, 128), F32),
                pltpu.VMEM((128, NB * 128), BF16),
                pltpu.VMEM((NB, 128, WINDOW), BF16),
                pltpu.VMEM((NB * EDGE, EROWS), BF16),
                pltpu.VMEM((NB, 256, 128), BF16),
                pltpu.VMEM((NB, EXPS, 4, 8, 128), F32),
                pltpu.VMEM((NB, 3, EXPS * EDGE, 128), F32),
                pltpu.VMEM((NB, COLS + 2 * PAD, 256), BF16),
                pltpu.VMEM((NB, EXPS * EDGE, COLS + 128), BF16),
                pltpu.VMEM((n_exp - 1, EXPS, ROWS, 128), BF16),
                pltpu.VMEM((n_exp - 1, EXPS, INNER, 128), BF16),
                pltpu.VMEM((n_exp - 1, EXPS, EDGE, 128), BF16),
                pltpu.VMEM((n_exp, EXPS, ROWS, 128), BF16),
                pltpu.VMEM((n_exp, EXPS, INNER, 128), BF16),
                pltpu.VMEM((n_exp, EXPS, EDGE, 128), BF16),
                pltpu.VMEM((n_exp, EXPS, ROWS, 128), F32),
                dma((5,)), dma((2,)), dma((2,)), dma((2,)),
                dma((n_exp,)), dma((n_exp,)), dma((n_exp,)), dma((n_exp,)), dma((n_exp,)), dma((n_exp,)),
            ],
            compiler_params=pltpu.CompilerParams(
                collective_id=0, has_side_effects=True, vmem_limit_bytes=60 * 1024 * 1024
            ),
            name="coadd",
        )(coeffs.transpose(1, 0, 2), degrees, footprint, masks, basis_taps, warped, variance)

    in_specs = (
        P("exp", "sky", None),
        P("exp", "sky", None),
        P(),
        P("exp", None, None),
        P("exp", None),
        P("exp", None),
        P("exp", "sky"),
    )
    return jax.shard_map(body, mesh=mesh, in_specs=in_specs, out_specs=P("sky", "exp"), check_vma=False)
```

time: 23.9 us -> 21.3 us (0.89)
  the two profiles are of different devices: /device:TPU:95 before, /device:TPU:64 now
where the time goes in v3:
time: 21.3 us; the launch traced here: 21.1 us
  Pallas kernels  19.7 us (92%)
  local copies, waits for them, and re-layouts  1.46 us (7%)
    pallas_call x1, Pallas kernels, body(): pl.pallas_call(functools.partial(kernel, n_sky, n_exp), out_shape=jax.Sha...  19.7 us
    unnamed x1, local copies, waits for them, and re-layouts  1.46 us

profile of v3, /device:TPU:64, one launch (start us, length us, event | category | flops | bytes accessed | tf_op | source)
XLA Modules:
  0.0 21.1 jit_solution(17275427205412001531)
XLA Ops:
  0.0 19.7 %coadd.1 = f32[120,128]{1,0:T(8,128)} custom-call(f32[9,2,10]{2,1,0:T(2,128)} %bitcast.1, s32[2,9]{1,0:T(2,128)} %degrees_hbm.1, s32[2,2]{1,0:T(2,128)} %footprint_hbm.1, s32[2,8]{1,0:T(2,128)} %masks_hbm.1, bf16[9,2,23]{2,1,0:T(2,128)(2,1)} %taps_hbm.1, bf16[2,120,1024]{2,1,0:T(8,128)(2,1)} %warped.1, bf16[2,120,1024]{2,1,0:T(8,128)(2,1)} %variance.1), custom_call_target="tpu_custom_call" | custom-call | tf_op jit(solution)/shard_map/coadd/pallas_call | solution.py:351
  19.7 1.5 %copy.9 = f32[120,128]{1,0:T(8,128)} copy(f32[120,128]{1,0:T(8,128)} %coadd.1) | data formatting | bytes 122880

commit v4 on v3

--- a/solution.py
+++ b/solution.py
@@ -20,6 +20,8 @@
 WINDOW = 160
 ORDERS = (0, 1, 1, 2, 2, 2, 3, 3, 3, 3)
 STEP = 16.0 / COLS
+RING = 4
+OFFSETS = ((0, 0), (2, 1), (2, 0), (1, 1), (3, 1), (0, 1), (1, 0), (3, 0))
 
 
 def iota(shape, dim):
@@ -35,7 +37,8 @@
 ):
     sky, me = lax.axis_index("sky"), lax.axis_index("exp")
     not_first, not_last = sky > 0, sky < n_sky - 1
-    peers = [lax.rem(me + t, n_exp) for t in range(n_exp)]
+    ring, pair = lax.rem(me, RING), me // RING
+    peers = [lax.rem(pair + dz, n_exp // RING) * RING + lax.rem(ring + dx, RING) for dx, dz in OFFSETS]
 
     barrier = pltpu.get_barrier_semaphore()
 
@@ -350,7 +353,7 @@
         dma = pltpu.SemaphoreType.DMA
         return pl.pallas_call(
             functools.partial(kernel, n_sky, n_exp),
-            out_shape=jax.ShapeDtypeStruct((ROWS, 128), F32),
+            out_shape=pltpu.VMEM((ROWS, 128), F32),
             in_specs=[hbm] * 7,
             out_specs=vmem,
             scratch_shapes=[

time: 21.3 us -> 19.9 us (0.934)
  local copies, waits for them, and re-layouts: 1.46 us -> 0.63 us
  Pallas kernels: 19.7 us -> 19.1 us
    unnamed x1, local copies, waits for them, and re-layouts: 1.46 us -> 0.63 us
    pallas_call x1, Pallas kernels: 19.7 us -> 19.1 us  [body(): pl.pallas_call(functools.partial(kernel, n_sky, n_exp), out_shape=pltpu.V...]
where the time goes in v4:
time: 19.9 us; the launch traced here: 19.8 us
  Pallas kernels  19.1 us (96%)
  local copies, waits for them, and re-layouts  0.63 us (3%)
    pallas_call x1, Pallas kernels, body(): pl.pallas_call(functools.partial(kernel, n_sky, n_exp), out_shape=pltpu.V...  19.1 us
    unnamed x1, local copies, waits for them, and re-layouts  0.63 us

profile of v4, /device:TPU:64, one launch (start us, length us, event | category | flops | bytes accessed | tf_op | source)
XLA Modules:
  0.0 19.8 jit_solution(16047511878871480665)
XLA Ops:
  0.0 19.1 %coadd.1 = f32[120,128]{1,0:T(8,128)S(1)} custom-call(f32[9,2,10]{2,1,0:T(2,128)} %bitcast.1, s32[2,9]{1,0:T(2,128)} %degrees_hbm.1, s32[2,2]{1,0:T(2,128)} %footprint_hbm.1, s32[2,8]{1,0:T(2,128)} %masks_hbm.1, bf16[9,2,23]{2,1,0:T(2,128)(2,1)} %taps_hbm.1, bf16[2,120,1024]{2,1,0:T(8,128)(2,1)} %warped.1, bf16[2,120,1024]{2,1,0:T(8,128)(2,1)} %variance.1), custom_call_target="tpu_custom_call" | custom-call | tf_op jit(solution)/shard_map/coadd/pallas_call | solution.py:354
  19.1 0.6 %copy.9 = f32[120,128]{1,0:T(8,128)} copy(f32[120,128]{1,0:T(8,128)S(1)} %coadd.1) | data formatting | bytes 122880

commit v5 on v4

--- a/solution.py
+++ b/solution.py
@@ -88,10 +88,12 @@
     k_row = jnp.where(low < ROWS, low - lane + HALF, -1)
     k_first = lane - low - (PAD - HALF)
     k_second = k_first + 128
+    tail = 96
     for b in range(NB):
         rowband[:, 128 * b : 128 * b + 128] = band(2 * b, k_row)
         colband[b, :, 0:128] = band(2 * b + 1, k_first)
-        colband[b, :, 128:WINDOW] = band(2 * b + 1, k_second)[:, 0 : WINDOW - 128]
+        colband[b, 0:tail, 128:WINDOW] = jnp.zeros((tail, WINDOW - 128), BF16)
+        colband[b, tail:128, 128:WINDOW] = band(2 * b + 1, k_second[tail:128])[:, 0 : WINDOW - 128]
 
     small[1].wait()
     small[2].wait()
@@ -225,18 +227,18 @@
     for t in range(1, n_exp):
         put_interior(msend.at[t - 1], peers[t])
         m_copies[t - 1].start()
-    put_interior(mrecv.at[0], peers[0])
 
     i_band, kappa = iota((EDGE, 128), 0), iota((EDGE, 128), 1)
     k_edge = (
         jnp.where(kappa < 48, kappa - HALO, kappa + 40) - jnp.where(i_band < LO, i_band, i_band + INNER) + HALF
     )
     k_edge = jnp.where(kappa < EROWS, k_edge, -1)
-    kappa_col, col = iota((256, 128), 0), iota((256, 128), 1)
-    k_edge_col = kappa_col - col - (64 - HALF)
+    k_edge_col = iota((160, 128), 0) + 48 - iota((160, 128), 1) - (64 - HALF)
     for b in range(NB):
         edge_rowband[EDGE * b : EDGE * b + EDGE, :] = band(2 * b, k_edge)[:, 0:EROWS]
-        edge_colband[b] = band(2 * b + 1, k_edge_col)
+        edge_colband[b, 0:48] = jnp.zeros((48, 128), BF16)
+        edge_colband[b, 48:208] = band(2 * b + 1, k_edge_col)
+        edge_colband[b, 208:256] = jnp.zeros((48, 128), BF16)
         for e in range(EXPS):
             g = cubic(coefficients(b, e), u_edge)
             for q in range(3):
@@ -259,12 +261,21 @@
         edge_image[e, 0:16, 64:1088] = halo[0, e]
         edge_image[e, 80:96, 64:1088] = halo[1, e]
 
-    for e in range(EXPS):
-        for n in range(5):
-            span = slice(256 * n, min(256 * n + 256, COLS + 128))
-            filtered = jnp.dot(edge_rowband[...], edge_image[e, :, span], preferred_element_type=F32).astype(BF16)
+    def put_filtered(tile, pieces):
+        filtered = jnp.dot(edge_rowband[...], tile, preferred_element_type=F32).astype(BF16)
+        for e, span, part in pieces:
             for b in range(NB):
-                edge_along[b, EDGE * e : EDGE * e + EDGE, span] = filtered[EDGE * b : EDGE * b + EDGE]
+                edge_along[b, EDGE * e : EDGE * e + EDGE, span] = filtered[EDGE * b : EDGE * b + EDGE, part]
+
+    for e in range(EXPS):
+        for n in range(4):
+            span = slice(256 * n, 256 * n + 256)
+            put_filtered(edge_image[e, :, span], [(e, span, slice(0, 256))])
+    rest = slice(COLS, COLS + 128)
+    put_filtered(
+        jnp.concatenate([edge_image[e, :, rest] for e in range(EXPS)], axis=1),
+        [(e, rest, slice(128 * e, 128 * e + 128)) for e in range(EXPS)],
+    )
 
     def put_edges(group):
         starts = [pl.multiple_of(peers[t] * 128, 128) for t in group]
@@ -288,6 +299,7 @@
 
     put_edges((1, 2, 3, 4))
     put_edges((5, 6, 7, 0))
+    put_interior(mrecv.at[0], peers[0])
 
     inner_chunks = ((0, 48), (48, INNER))
     for t in range(n_exp):

time: 19.9 us -> 19.9 us (level)
  no operation moved by 1% of the time
where the time goes in v5:
time: 19.9 us; the launch traced here: 19.8 us
  Pallas kernels  19.2 us (96%)
  local copies, waits for them, and re-layouts  0.63 us (3%)
    pallas_call x1, Pallas kernels, body(): pl.pallas_call(functools.partial(kernel, n_sky, n_exp), out_shape=pltpu.V...  19.2 us
    unnamed x1, local copies, waits for them, and re-layouts  0.63 us

profile of v5, /device:TPU:64, one launch (start us, length us, event | category | flops | bytes accessed | tf_op | source)
XLA Modules:
  0.0 19.8 jit_solution(7356771968506012698)
XLA Ops:
  0.0 19.2 %coadd.1 = f32[120,128]{1,0:T(8,128)S(1)} custom-call(f32[9,2,10]{2,1,0:T(2,128)} %bitcast.1, s32[2,9]{1,0:T(2,128)} %degrees_hbm.1, s32[2,2]{1,0:T(2,128)} %footprint_hbm.1, s32[2,8]{1,0:T(2,128)} %masks_hbm.1, bf16[9,2,23]{2,1,0:T(2,128)(2,1)} %taps_hbm.1, bf16[2,120,1024]{2,1,0:T(8,128)(2,1)} %warped.1, bf16[2,120,1024]{2,1,0:T(8,128)(2,1)} %variance.1), custom_call_target="tpu_custom_call" | custom-call | tf_op jit(solution)/shard_map/coadd/pallas_call | solution.py:366
  19.2 0.6 %copy.9 = f32[120,128]{1,0:T(8,128)} copy(f32[120,128]{1,0:T(8,128)S(1)} %coadd.1) | data formatting | bytes 122880

commit v6 on v5

--- a/solution.py
+++ b/solution.py
@@ -119,15 +119,16 @@
             else:
                 vsend[t - 1, e] = masked
 
+    own_copy.wait()
     n_neighbours = not_first.astype(jnp.int32) + not_last.astype(jnp.int32)
     pl.semaphore_wait(barrier, n_exp - 1 + n_neighbours)
 
     down = pltpu.make_async_remote_copy(
-        src_ref=warped.at[:, ROWS - HALO : ROWS, :], dst_ref=halo.at[0],
+        src_ref=own.at[:, ROWS - HALO : ROWS, :], dst_ref=halo.at[0],
         send_sem=halo_send.at[0], recv_sem=halo_recv.at[0], device_id=(sky + 1, me), device_id_type=MESH,
     )
     up = pltpu.make_async_remote_copy(
-        src_ref=warped.at[:, 0:HALO, :], dst_ref=halo.at[1],
+        src_ref=own.at[:, 0:HALO, :], dst_ref=halo.at[1],
         send_sem=halo_send.at[1], recv_sem=halo_recv.at[1], device_id=(sky - 1, me), device_id_type=MESH,
     )
 
@@ -176,7 +177,6 @@
     for b in range(NB):
         along[b, 0:PAD, :] = jnp.zeros((PAD, 256), BF16)
         along[b, PAD + COLS : COLS + 2 * PAD, :] = jnp.zeros((PAD, 256), BF16)
-    own_copy.wait()
     for e in range(EXPS):
         for i in range(COLS // 128):
             span = slice(128 * i, 128 * i + 128)

time: 19.9 us -> 19.9 us (level)
  no operation moved by 1% of the time
where the time goes in v6:
time: 19.9 us
  Pallas kernels  19.2 us (96%)
  local copies, waits for them, and re-layouts  0.63 us (3%)
    pallas_call x1, Pallas kernels, body(): pl.pallas_call(functools.partial(kernel, n_sky, n_exp), out_shape=pltpu.V...  19.2 us
    unnamed x1, local copies, waits for them, and re-layouts  0.63 us

profile of v6, /device:TPU:64, one launch (start us, length us, event | category | flops | bytes accessed | tf_op | source)
XLA Modules:
  0.0 19.9 jit_solution(7057583057859626459)
XLA Ops:
  0.0 19.2 %coadd.1 = f32[120,128]{1,0:T(8,128)S(1)} custom-call(f32[9,2,10]{2,1,0:T(2,128)} %bitcast.1, s32[2,9]{1,0:T(2,128)} %degrees_hbm.1, s32[2,2]{1,0:T(2,128)} %footprint_hbm.1, s32[2,8]{1,0:T(2,128)} %masks_hbm.1, bf16[9,2,23]{2,1,0:T(2,128)(2,1)} %taps_hbm.1, bf16[2,120,1024]{2,1,0:T(8,128)(2,1)} %warped.1, bf16[2,120,1024]{2,1,0:T(8,128)(2,1)} %variance.1), custom_call_target="tpu_custom_call" | custom-call | tf_op jit(solution)/shard_map/coadd/pallas_call | solution.py:366
  19.2 0.6 %copy.9 = f32[120,128]{1,0:T(8,128)} copy(f32[120,128]{1,0:T(8,128)S(1)} %coadd.1) | data formatting | bytes 122880
